TPU v7x, 128 devices: a whole 4x4x4 slice. The times are simulated.
128 devices in a mesh: blk: 32 (over x, z, core), tok: 4 (over y).
Axes of the slice: x: 4, y: 4, z: 4, core: 2. Of those that a mesh axis runs over, the one named last changes fastest.
Arguments:
- stream: bfloat16 [16384, 1664], P(('tok', 'blk'))
- queries: bfloat16 [16384, 1664], P(('tok', 'blk'))
- key_cache: bfloat16 [16384, 1664], P(('tok', 'blk'))
- value_cache: bfloat16 [16384, 1664], P(('tok', 'blk')), may hold values from -6 to 6
- segments: int32 [16384], P('tok'), may hold values from 63 to 16383, as said below
- stale_rows: int32 [1536], P(('tok', 'blk')), may hold values from 0 to 16383, as said below
- owners: int32 [4096], P(('tok', 'blk')), may hold values from 0 to 3, as said below
- attn_gain: float32 [1664], replicated, may hold values from 0.1 to 1.9
- w_key: bfloat16 [1664, 1664], replicated, may hold values from -0.15625 to 0.15625
- key_bias: float32 [1664], replicated, may hold values from -3 to 3
- mlp_gain: float32 [1664], replicated, may hold values from 0.1 to 1.9
- w_fc: bfloat16 [1664, 8192], P(None, 'blk'), may hold values from -0.15625 to 0.15625
- b_fc: float32 [8192], P('blk'), may hold values from -3 to 3
- w_proj: bfloat16 [8192, 1664], P('blk'), may hold values from -0.125 to 0.125
- b_proj: float32 [1664], replicated, may hold values from -3 to 3
- merge_gain: float32 [1664], replicated, may hold values from 0.1 to 1.9
- w_merge: bfloat16 [1664, 1664], replicated, may hold values from -0.15625 to 0.15625
- b_merge: float32 [1664], replicated, may hold values from -3 to 3
Outputs:
- refreshed_keys: bfloat16 [16384, 1664], P(('tok', 'blk'))
- delivered: bfloat16 [4, 32, 128, 1664], P('tok', 'blk')
Inputs may be any that keep to these rules, and one draw needn't show every extreme that they name: `segments`: A segment's id is the index of its last row, so ids never fall; each segment has 4 to 128 rows, a multiple of 4, and lies inside one aligned block of 4096 rows; each such block begins with a segment of 64 rows followed by one of exactly 128 rows. `stale_rows`: Distinct; the aligned block of 128 rows of each device holds exactly 12 of them, all inside that block and listed on that device; row 0 and the last row are always listed. `owners`: all merged tokens of one segment (the segment of row 4 m for merged token m) have the same owner.
All inputs are finite; a program needn't handle non-finite values.
Results may differ from a plain program's by a relative error of at most 0.011.
Values may be sent and summed in bfloat16 or wider, within the bound.
No kernel may reach another device: no remote copies, remote signals or barrier semaphores. Data moves between devices by JAX's collectives and lax.ppermute only.
A program may use at most 192 MiB of HBM per device.

v0:
```python
import jax
import jax.numpy as jnp
from jax import lax
from jax.sharding import PartitionSpec as P

HEADS = 16


def passed_along(block, axis, distance):
    devices = range(lax.axis_size(axis))
    route = [(i - distance, i) for i in devices if i - distance in devices]
    return lax.ppermute(block, axis, route)


def layer_norm(values, gain):
    center = values - jnp.mean(values, axis=-1, keepdims=True)
    spread = jnp.mean(center * center, axis=-1, keepdims=True)
    return center * lax.rsqrt(spread + 1e-06) * gain


def body(
    stream,
    queries,
    key_cache,
    value_cache,
    segments,
    stale_rows,
    owners,
    attn_gain,
    w_key,
    key_bias,
    mlp_gain,
    w_fc,
    b_fc,
    w_proj,
    b_proj,
    merge_gain,
    w_merge,
    b_merge,
):
    row_count = stream.shape[0]
    model_width = stream.shape[1]
    head_size = model_width // HEADS
    local_rows = stale_rows % row_count
    held = layer_norm(stream[local_rows].astype(jnp.float32), attn_gain).astype(jnp.bfloat16)
    fresh_keys = (jnp.dot(held, w_key, preferred_element_type=jnp.float32) + key_bias).astype(
        jnp.bfloat16
    )
    refreshed = key_cache.at[local_rows].set(fresh_keys)
    below = passed_along((refreshed, value_cache), "blk", 1)
    above = passed_along((refreshed, value_cache), "blk", -1)
    key_window = jnp.concatenate([below[0], refreshed, above[0]], axis=0).reshape(
        3 * row_count, HEADS, head_size
    )
    value_window = jnp.concatenate([below[1], value_cache, above[1]], axis=0).reshape(
        3 * row_count, HEADS, head_size
    )
    position = lax.axis_index("blk")
    minus_ones = jnp.full((row_count,), -1, jnp.int32)
    seg_padded = jnp.concatenate([minus_ones, segments, minus_ones], axis=0)
    key_seg = lax.dynamic_slice_in_dim(seg_padded, position * row_count, 3 * row_count, 0)
    query_seg = lax.dynamic_slice_in_dim(segments, position * row_count, row_count, 0)
    query_heads = queries.reshape(row_count, HEADS, head_size)
    scores = jnp.einsum(
        "qhd,khd->hqk", query_heads, key_window, preferred_element_type=jnp.float32
    ) * (1.0 / head_size**0.5)
    allowed = (query_seg[:, None] == key_seg[None, :])[None]
    scores = jnp.where(allowed, scores, -jnp.inf)
    top_score = jnp.max(scores, axis=-1, keepdims=True)
    weights = jnp.exp(scores - top_score)
    probs = (weights / jnp.sum(weights, axis=-1, keepdims=True)).astype(jnp.bfloat16)
    attended = jnp.einsum("hqk,khd->qhd", probs, value_window, preferred_element_type=jnp.float32)
    attended = attended.reshape(row_count, model_width).astype(jnp.bfloat16)
    mixed = stream.astype(jnp.float32) + attended.astype(jnp.float32)
    normed = layer_norm(mixed, mlp_gain).astype(jnp.bfloat16)
    group_units = jax.nn.gelu(
        jnp.dot(
            lax.all_gather(normed, "blk", axis=0, tiled=True),
            w_fc,
            preferred_element_type=jnp.float32,
        )
        + b_fc,
        approximate=False,
    ).astype(jnp.bfloat16)
    summed = lax.psum_scatter(
        jnp.dot(group_units, w_proj, preferred_element_type=jnp.float32).astype(jnp.bfloat16),
        "blk",
        scatter_dimension=0,
        tiled=True,
    ).astype(jnp.float32)
    pooled = jnp.mean((mixed + summed).reshape(row_count // 4, 4, model_width), axis=1) + b_proj
    merge_in = layer_norm(pooled, merge_gain).astype(jnp.bfloat16)
    merged = (jnp.dot(merge_in, w_merge, preferred_element_type=jnp.float32) + b_merge).astype(
        jnp.bfloat16
    )
    owner_count = lax.axis_size("tok")
    merged_rows = row_count // 4
    owner_hot = (owners[:, None] == jnp.arange(owner_count, dtype=jnp.int32)[None, :]).astype(
        jnp.int32
    )
    ranking = jnp.sum(jnp.cumsum(owner_hot, axis=0) * owner_hot, axis=-1) - 1
    selector = (
        owners[None, None, :] == jnp.arange(owner_count, dtype=jnp.int32)[:, None, None]
    ) & (ranking[None, None, :] == jnp.arange(merged_rows, dtype=jnp.int32)[None, :, None])
    outgoing = jnp.einsum(
        "osm,md->osd", selector.astype(jnp.bfloat16), merged, preferred_element_type=jnp.float32
    ).astype(jnp.bfloat16)
    arrived = lax.all_to_all(outgoing, "tok", split_axis=0, concat_axis=0, tiled=True)
    delivered = arrived.reshape(1, 1, owner_count * merged_rows, model_width)
    return (refreshed, delivered)


def solution(mesh):
    return jax.shard_map(
        body,
        mesh=mesh,
        in_specs=(
            P(("tok", "blk"), None),
            P(("tok", "blk"), None),
            P(("tok", "blk"), None),
            P(("tok", "blk"), None),
            P("tok"),
            P(("tok", "blk")),
            P(("tok", "blk")),
            P(),
            P(),
            P(),
            P(),
            P(None, "blk"),
            P("blk"),
            P("blk", None),
            P(),
            P(),
            P(),
            P(),
        ),
        out_specs=(P(("tok", "blk"), None), P("tok", "blk", None, None)),
        check_vma=False,
    )
```

profile of v0, /device:TPU:0, one launch (start us, length us, event | category | flops | bytes accessed | tf_op | source)
XLA Modules:
  0.0 274.7 jit_solution(774383592987161788)
XLA Ops:
  7.3 0.8 compare_select_fusion
  8.1 1.7 gather_fusion
  10.1 3.4 %fusion.14 = bf16[12,1664]{1,0:T(8,128)(2,1)S(1)} fusion(bf16[1664,1664]{1,0:T(8,128)(2,1)} %param.26, bf16[12,1664]{1,0:T(8,128)(2,1)S(1)} %gather_fusion, f32[1664]{0:T(1024)} %param.27, f32[1664]{0:T(1024)} %param.25, f32[12]{0:T(128)S(1)} %add_rsqrt_fusion.2, f32[12]{0:T(128)S(1)} %broadcast_multiply_fusion.2), kind=kOutput, calls=%fused_computation.33 | convolution fusion | flops 66593280 | bytes 5631072 | tf_op jit(solution)/shard_map/dot_general | solution.py:46
  13.6 0.9 scatter_fusion
  14.5 1.3 collective-permute-start.2
  15.9 1.3 collective-permute-start.3
  17.2 5.3 %collective-permute-start = (bf16[128,1664]{1,0:T(8,128)(2,1)S(1)}, bf16[128,1664]{1,0:T(8,128)(2,1)S(1)}, u32[]{:S(2)}, u32[]{:S(2)}) collective-permute-start(bf16[128,1664]{1,0:T(8,128)(2,1)S(1)} %copy-done.5), channel_id=1, source_target_pairs={{0,4},{4,8},{8,12},{12,16},{16,20},{20,24},{24,28},{28,32},{32,36}... | collective-permute-start | bytes 1277960 | tf_op jit(solution)/shard_map/ppermute | solution.py:12
  22.4 1.3 collective-permute-start.1
  23.8 1.0 copy.32
  25.1 0.7 copy-done.6
  25.8 1.2 pad_maximum_fusion.1
  27.0 1.5 copy.31
  28.6 1.1 pad_maximum_fusion
  29.7 1.6 copy.30
  31.3 4.4 %fusion.118 = (f32[16,128]{1,0:T(8,128)S(1)}, f32[16,128,384]{1,2,0:T(8,128)}) fusion(pred[128,384]{0,1:T(8,128)(4,1)S(1)} %broadcast_compare_fusion, bf16[384,16,104]{0,2,1:T(8,128)(2,1)} %bitcast.33, bf16[128,16,104]{0,2,1:T(8,128)(2,1)} %bitcast.36), kind=kOutput, calls=%fused_computation.159 | convolution fusion | flops 166723968 | bytes 4907008 | tf_op jit(solution)/shard_map/sub | solution.py:70
  35.7 2.5 fusion.52
  39.0 1.0 multiply_convert_fusion
  40.2 74.5 %all-gather.2.cloned.1.call-done = bf16[4096,1664]{1,0:T(8,128)(2,1)} async-done(((bf16[128,1664]{1,0:T(8,128)(2,1)}), bf16[4096,1664]{1,0:T(8,128)(2,1)}) %all-gather.2.cloned.1.call-update) | async-done | bytes 13631504 | tf_op jit(solution)/shard_map/all_gather | solution.py:78
  114.7 27.8 %convolution_convert_fusion = bf16[4096,1664]{1,0:T(8,128)(2,1)} fusion(bf16[256,1664]{1,0:T(8,128)(2,1)S(1)} %copy-done, bf16[4096,1664]{1,0:T(8,128)(2,1)} %all-gather.2.cloned.1.call-done, bf16[1664,256]{1,0:T(8,128)(2,1)S(1)} %copy-done.14, f32[256]{0:T(256)S(1)} %copy-done.15), kind=kOutput, calls=%fused_computation.3 | convolution fusion | flops 7055343616 | bytes 28967936 | tf_op jit(solution)/shard_map/dot_general | solution.py:86
  143.6 105.9 %reduce-scatter.2.cloned.1.call-done = bf16[128,1664]{1,0:T(8,128)(2,1)} async-done(((bf16[4096,1664]{1,0:T(8,128)(2,1)}), bf16[128,1664]{1,0:T(8,128)(2,1)}) %reduce-scatter.2.cloned.1.call-update) | async-done | bytes 426000 | tf_op jit(solution)/shard_map/reduce_scatter | solution.py:85
  249.4 1.1 convert_add_fusion
  251.7 3.8 %convolution_convert_fusion.1 = bf16[4,32,1664]{2,1,0:T(8,128)(2,1)S(1)} fusion(bf16[1664,1664]{1,0:T(8,128)(2,1)} %param.34, f32[32,1664]{1,0:T(8,128)S(1)} %reduce_sum.87, f32[1664]{0:T(1024)S(1)} %copy-done.11, f32[1664]{0:T(1024)S(1)} %copy-done.12, f32[32]{0:T(128)S(1)} %add_rsqrt_fusion, f32[32]{0:T(128)S(1)} %broadcast_multiply_fusion, ...), kind=kOutput, calls=%fused_computation.27 | convolution fusion | flops 191483904 | bytes 6198144 | tf_op jit(solution)/shard_map/osm,md->osd/dot_general | solution.py:105
  255.5 11.6 %all_to_all.5 = bf16[4,32,1664]{2,1,0:T(8,128)(2,1)S(1)} all-to-all(bf16[4,32,1664]{2,1,0:T(8,128)(2,1)S(1)} %convolution_convert_fusion.1), channel_id=1, replica_groups=mesh['blk'=32,'tok'=4] {'tok'}, dimensions={0} | all-to-all | bytes 851968 | tf_op jit(solution)/shard_map/all_to_all | solution.py:108
  267.1 0.8 copy.40
  (65 shorter events, 3.8 us)
Async XLA Ops:
  7.2 107.6 %copy-start = (bf16[256,1664]{1,0:T(8,128)(2,1)S(1)}, bf16[256,1664]{1,0:T(8,128)(2,1)}, u32[]{:S(2)}) copy-start(bf16[256,1664]{1,0:T(8,128)(2,1)} %param.31) | copy-start | bytes 2555908
  7.2 16.6 %copy-start.7 = (bf16[128,1664]{1,0:T(8,128)(2,1)S(1)}, bf16[128,1664]{1,0:T(8,128)(2,1)}, u32[]{:S(2)}) copy-start(bf16[128,1664]{1,0:T(8,128)(2,1)} %param.19) | copy-start | bytes 1277956
  7.2 6.4 %copy-start.3 = (bf16[128,1664]{1,0:T(8,128)(2,1)S(1)}, bf16[128,1664]{1,0:T(8,128)(2,1)}, u32[]{:S(2)}) copy-start(bf16[128,1664]{1,0:T(8,128)(2,1)} %param.20) | copy-start | bytes 1277956
  7.2 10.0 %copy-start.5 = (bf16[128,1664]{1,0:T(8,128)(2,1)S(1)}, bf16[128,1664]{1,0:T(8,128)(2,1)}, u32[]{:S(2)}) copy-start(bf16[128,1664]{1,0:T(8,128)(2,1)} %param.21) | copy-start | bytes 1277956
  7.2 107.5 %all-gather.2.cloned.1.call-start = ((), (), s32[]{:S(2)}) async-start(), calls=%async_computation.2 | async-start | bytes 14057472 | tf_op jit(solution)/shard_map/all_gather | solution.py:78
  7.3 17.5 %copy-start.9 = (s32[4096]{0:T(1024)S(1)}, s32[4096]{0:T(1024)}, u32[]{:S(2)}) copy-start(s32[4096]{0:T(1024)} %param.22) | copy-start | bytes 49156
  14.5 15.2 %copy-start.2 = (bf16[128,1664]{1,0:T(8,128)(2,1)}, bf16[128,1664]{1,0:T(8,128)(2,1)S(1)}, u32[]{:S(2)}) copy-start(bf16[128,1664]{1,0:T(8,128)(2,1)S(1)} %scatter_fusion) | copy-start | bytes 1277956
  14.5 10.5 %collective-permute-start.2 = (bf16[128,1664]{1,0:T(8,128)(2,1)S(1)}, bf16[128,1664]{1,0:T(8,128)(2,1)S(1)}, u32[]{:S(2)}, u32[]{:S(2)}) collective-permute-start(bf16[128,1664]{1,0:T(8,128)(2,1)S(1)} %scatter_fusion), channel_id=1, source_target_pairs={{0,4},{4,8},{8,12},{12,16},{16,20},{20,24},{24,28},{28,32},{32,36}... | collective-permute-start | bytes 1277960 | tf_op jit(solution)/shard_map/ppermute | solution.py:12
  15.9 9.9 %collective-permute-start.3 = (bf16[128,1664]{1,0:T(8,128)(2,1)S(1)}, bf16[128,1664]{1,0:T(8,128)(2,1)}, u32[]{:S(2)}, u32[]{:S(2)}) collective-permute-start(bf16[128,1664]{1,0:T(8,128)(2,1)S(1)} %scatter_fusion), channel_id=1, source_target_pairs={{4,0},{8,4},{12,8},{16,12},{20,16},{24,20},{28,24},{32,28},{36,32}... | collective-permute-start | bytes 1277960 | tf_op jit(solution)/shard_map/ppermute | solution.py:12
  17.2 11.4 %collective-permute-start = (bf16[128,1664]{1,0:T(8,128)(2,1)S(1)}, bf16[128,1664]{1,0:T(8,128)(2,1)S(1)}, u32[]{:S(2)}, u32[]{:S(2)}) collective-permute-start(bf16[128,1664]{1,0:T(8,128)(2,1)S(1)} %copy-done.5), channel_id=1, source_target_pairs={{0,4},{4,8},{8,12},{12,16},{16,20},{20,24},{24,28},{28,32},{32,36}... | collective-permute-start | bytes 1277960 | tf_op jit(solution)/shard_map/ppermute | solution.py:12
  22.4 6.1 %collective-permute-start.1 = (bf16[128,1664]{1,0:T(8,128)(2,1)S(1)}, bf16[128,1664]{1,0:T(8,128)(2,1)}, u32[]{:S(2)}, u32[]{:S(2)}) collective-permute-start(bf16[128,1664]{1,0:T(8,128)(2,1)S(1)} %copy-done.5), channel_id=1, source_target_pairs={{4,0},{8,4},{12,8},{16,12},{20,16},{24,20},{28,24},{32,28},{36,32}... | collective-permute-start | bytes 1277960 | tf_op jit(solution)/shard_map/ppermute | solution.py:12
  25.0 0.8 copy-start.6
  31.3 4.4 %copy-start.4 = (bf16[384,1664]{0,1:T(8,128)(2,1)S(1)}, bf16[384,1664]{0,1:T(8,128)(2,1)}, u32[]{:S(2)}) copy-start(bf16[384,1664]{0,1:T(8,128)(2,1)} %copy.30) | copy-start | bytes 3833860
  35.7 2.9 %copy-start.1 = (bf16[128,1664]{1,0:T(8,128)(2,1)S(1)}, bf16[128,1664]{1,0:T(8,128)(2,1)}, u32[]{:S(2)}) copy-start(bf16[128,1664]{1,0:T(8,128)(2,1)} %param.18) | copy-start | bytes 1277956
  38.2 0.8 copy-start.10
  38.2 76.5 %copy-start.15 = (f32[256]{0:T(256)S(1)}, f32[256]{0:T(256)}, u32[]{:S(2)}) copy-start(f32[256]{0:T(256)} %param.30) | copy-start | bytes 3076
  38.5 76.2 %copy-start.14 = (bf16[1664,256]{1,0:T(8,128)(2,1)S(1)}, bf16[1664,256]{1,0:T(8,128)(2,1)}, u32[]{:S(2)}) copy-start(bf16[1664,256]{1,0:T(8,128)(2,1)} %param.29) | copy-start | bytes 2555908
  40.0 209.4 %reduce-scatter.2.cloned.1.call-start = ((), (), s32[]{:S(2)}) async-start(), calls=%async_computation.3 | async-start | bytes 14057472 | tf_op jit(solution)/shard_map/reduce_scatter | solution.py:85
  142.6 0.7 copy-start.13
  143.2 108.1 %copy-start.8 = (f32[1664]{0:T(1024)S(1)}, f32[1664]{0:T(1024)}, u32[]{:S(2)}) copy-start(f32[1664]{0:T(1024)} %param.32) | copy-start | bytes 19972
  143.2 108.5 %copy-start.11 = (f32[1664]{0:T(1024)S(1)}, f32[1664]{0:T(1024)}, u32[]{:S(2)}) copy-start(f32[1664]{0:T(1024)} %param.35) | copy-start | bytes 19972
  143.2 108.5 %copy-start.12 = (f32[1664]{0:T(1024)S(1)}, f32[1664]{0:T(1024)}, u32[]{:S(2)}) copy-start(f32[1664]{0:T(1024)} %param.33) | copy-start | bytes 19972
Sparse Core Ops, SparseCore 0:
  40.1 74.5 all-gather.1
  142.7 106.6 reduce-scatter.1
where the time goes:
time: 275 us
  waiting for transfers between devices  180 us (65%)
  matrix products  42 us (15%)
  between operations  14.3 us (5%)
  blocking collectives  11.6 us (4%)
  local copies, waits for them, and re-layouts  9.54 us (3%)
  starting transfers between devices  9.43 us (3%)
  other arithmetic  7.38 us (3%)
    reduce_scatter x1, waiting for transfers between devices, body(): lax.psum_scatter(jnp.dot(group_units, w_proj, preferred_element_type=jnp....  106 us
    all_gather x1, waiting for transfers between devices, body(): lax.all_gather(normed, 'blk', axis=0, tiled=True)  74.5 us
    dot_general x1, matrix products, body(): jnp.dot(group_units, w_proj, preferred_element_type=jnp.float32)  27.8 us
    all_to_all x1, blocking collectives, body(): lax.all_to_all(outgoing, 'tok', split_axis=0, concat_axis=0, tiled=True)  11.6 us
    ppermute x4, starting transfers between devices, passed_along(): return lax.ppermute(block, axis, route)  9.17 us
  transfers between devices with their start and end apart: 6, of which 2 were waited for; matrix products, arithmetic and copies ran while one was open for 2% of the time, Pallas kernels for 0%

commit v1 on v0

--- a/solution.py
+++ b/solution.py
@@ -2,6 +2,7 @@
 import jax.numpy as jnp
 from jax import lax
 from jax.sharding import PartitionSpec as P
+from jax.lax import all_to_all, axis_size
 
 HEADS = 16
 
@@ -73,13 +74,19 @@
     attended = attended.reshape(row_count, model_width).astype(jnp.bfloat16)
     mixed = stream.astype(jnp.float32) + attended.astype(jnp.float32)
     normed = layer_norm(mixed, mlp_gain).astype(jnp.bfloat16)
+
+    def trails_see(obj, on_dim):
+        amount_of = axis_size("blk")
+        return all_to_all(
+            jnp.tile(obj, [amount_of if c == on_dim else 1 for c in range(obj.ndim)]),
+            "blk",
+            split_axis=on_dim,
+            concat_axis=on_dim,
+            tiled=True,
+        )
+
     group_units = jax.nn.gelu(
-        jnp.dot(
-            lax.all_gather(normed, "blk", axis=0, tiled=True),
-            w_fc,
-            preferred_element_type=jnp.float32,
-        )
-        + b_fc,
+        jnp.dot(trails_see(normed, 0), w_fc, preferred_element_type=jnp.float32) + b_fc,
         approximate=False,
     ).astype(jnp.bfloat16)
     summed = lax.psum_scatter(

time: 275 us -> 372 us (1.35)
  blocking collectives: 11.6 us -> 179 us
  waiting for transfers between devices: 180 us -> 105 us
  local copies, waits for them, and re-layouts: 9.54 us -> 16.1 us
    all_to_all x0 -> x1, blocking collectives: none -> 167 us  [trails_see(): all_to_all(jnp.tile(obj, [amount_of if c == on_dim else 1 for c in range(...]
    all_gather x1 -> x0, waiting for transfers between devices: 74.5 us -> none  [body(): lax.all_gather(normed, 'blk', axis=0, tiled=True)]
    another operation x0 -> x1, local copies, waits for them, and re-layouts: none -> 6.59 us  [trails_see(): jnp.tile(obj, [amount_of if c == on_dim else 1 for c in range(obj.ndim)])]
  transfers between devices with their start and end apart: 6 -> 5, of which waited for: 2 -> 1; matrix products, arithmetic and copies ran while one was open for 2% -> 1% of each run, Pallas kernels for 0% -> 0%
where the time goes in v1:
time: 372 us
  blocking collectives  179 us (48%)
  waiting for transfers between devices  105 us (28%)
  matrix products  42 us (11%)
  local copies, waits for them, and re-layouts  16.1 us (4%)
  between operations  14.3 us (4%)
  starting transfers between devices  9.21 us (2%)
  other arithmetic  6.62 us (2%)
    all_to_all x1, blocking collectives, trails_see(): all_to_all(jnp.tile(obj, [amount_of if c == on_dim else 1 for c in range(...  167 us
    reduce_scatter x1, waiting for transfers between devices, body(): lax.psum_scatter(jnp.dot(group_units, w_proj, preferred_element_type=jnp....  105 us
    dot_general x1, matrix products, body(): jnp.dot(group_units, w_proj, preferred_element_type=jnp.float32)  27.8 us
    all_to_all x1, blocking collectives, body(): lax.all_to_all(outgoing, 'tok', split_axis=0, concat_axis=0, tiled=True)  11.6 us
    ppermute x4, starting transfers between devices, passed_along(): return lax.ppermute(block, axis, route)  9.17 us
  transfers between devices with their start and end apart: 5, of which 1 were waited for; matrix products, arithmetic and copies ran while one was open for 1% of the time, Pallas kernels for 0%

profile of v1, /device:TPU:0, one launch (start us, length us, event | category | flops | bytes accessed | tf_op | source)
XLA Modules:
  0.0 371.5 jit_solution(14682407387627105649)
XLA Ops:
  7.3 0.8 compare_select_fusion
  8.1 1.7 gather_fusion
  10.1 3.4 fusion.14
  13.6 0.9 scatter_fusion
  14.5 1.3 collective-permute-start.2
  15.9 1.3 collective-permute-start.3
  17.2 5.3 %collective-permute-start = (bf16[128,1664]{1,0:T(8,128)(2,1)S(1)}, bf16[128,1664]{1,0:T(8,128)(2,1)S(1)}, u32[]{:S(2)}, u32[]{:S(2)}) collective-permute-start(bf16[128,1664]{1,0:T(8,128)(2,1)S(1)} %copy-done.6), channel_id=1, source_target_pairs={{0,4},{4,8},{8,12},{12,16},{16,20},{20,24},{24,28},{28,32},{32,36}... | collective-permute-start | bytes 1277960 | tf_op jit(solution)/shard_map/ppermute | solution.py:13
  22.4 1.3 collective-permute-start.1
  23.8 1.0 copy.32
  25.1 0.7 copy-done.7
  25.8 1.2 pad_maximum_fusion.1
  27.0 1.5 copy.31
  28.6 1.1 pad_maximum_fusion
  29.7 1.6 copy.30
  31.3 4.4 %fusion.118 = (f32[16,128]{1,0:T(8,128)S(1)}, f32[16,128,384]{1,2,0:T(8,128)}) fusion(pred[128,384]{0,1:T(8,128)(4,1)S(1)} %broadcast_compare_fusion, bf16[384,16,104]{0,2,1:T(8,128)(2,1)} %bitcast.35, bf16[128,16,104]{0,2,1:T(8,128)(2,1)} %bitcast.38), kind=kOutput, calls=%fused_computation.159 | convolution fusion | flops 166723968 | bytes 4907008 | tf_op jit(solution)/shard_map/sub | solution.py:71
  35.7 2.5 fusion.52
  39.2 6.6 %tile.2 = bf16[32,128,1664]{2,1,0:T(8,128)(2,1)} broadcast(bf16[128,1664]{1,0:T(8,128)(2,1)S(1)} %multiply_convert_fusion), dimensions={1,2} | broadcast | bytes 14057472 | tf_op jit(solution)/shard_map/tile | solution.py:81
  45.8 166.9 %all_to_all.14 = bf16[32,128,1664]{2,1,0:T(8,128)(2,1)} all-to-all(bf16[32,128,1664]{2,1,0:T(8,128)(2,1)} %tile.2), channel_id=1, replica_groups=mesh['blk'=32,'tok'=4] {'blk'}, dimensions={0} | all-to-all | bytes 27262976 | tf_op jit(solution)/shard_map/all_to_all | solution.py:80
  212.7 27.8 %convolution_convert_fusion = bf16[4096,1664]{1,0:T(8,128)(2,1)} fusion(bf16[256,1664]{1,0:T(8,128)(2,1)S(1)} %copy-done, bf16[4096,1664]{1,0:T(8,128)(2,1)} %bitcast.33, bf16[1664,256]{1,0:T(8,128)(2,1)S(1)} %copy-done.15, f32[256]{0:T(256)S(1)} %copy-done.16), kind=kOutput, calls=%fused_computation.3 | convolution fusion | flops 7055343616 | bytes 28967936 | tf_op jit(solution)/shard_map/dot_general | solution.py:93
  241.5 104.7 %reduce-scatter.2.cloned.1.call-done = bf16[128,1664]{1,0:T(8,128)(2,1)} async-done(((bf16[4096,1664]{1,0:T(8,128)(2,1)}), bf16[128,1664]{1,0:T(8,128)(2,1)}) %reduce-scatter.2.cloned.1.call-update) | async-done | bytes 426000 | tf_op jit(solution)/shard_map/reduce_scatter | solution.py:92
  346.2 1.1 convert_add_fusion
  348.5 3.8 %convolution_convert_fusion.1 = bf16[4,32,1664]{2,1,0:T(8,128)(2,1)S(1)} fusion(bf16[1664,1664]{1,0:T(8,128)(2,1)} %param.34, f32[32,1664]{1,0:T(8,128)S(1)} %reduce_sum.87, f32[1664]{0:T(1024)S(1)} %copy-done.12, f32[1664]{0:T(1024)S(1)} %copy-done.13, f32[32]{0:T(128)S(1)} %add_rsqrt_fusion, f32[32]{0:T(128)S(1)} %broadcast_multiply_fusion, ...), kind=kOutput, calls=%fused_computation.27 | convolution fusion | flops 191483904 | bytes 6198144 | tf_op jit(solution)/shard_map/osm,md->osd/dot_general | solution.py:112
  352.3 11.6 %all_to_all.15 = bf16[4,32,1664]{2,1,0:T(8,128)(2,1)S(1)} all-to-all(bf16[4,32,1664]{2,1,0:T(8,128)(2,1)S(1)} %convolution_convert_fusion.1), channel_id=1, replica_groups=mesh['blk'=32,'tok'=4] {'tok'}, dimensions={0} | all-to-all | bytes 851968 | tf_op jit(solution)/shard_map/all_to_all | solution.py:115
  363.9 0.8 copy.40
  (66 shorter events, 3.8 us)
Async XLA Ops:
  7.2 205.5 %copy-start = (bf16[256,1664]{1,0:T(8,128)(2,1)S(1)}, bf16[256,1664]{1,0:T(8,128)(2,1)}, u32[]{:S(2)}) copy-start(bf16[256,1664]{1,0:T(8,128)(2,1)} %param.31) | copy-start | bytes 2555908
  7.2 16.6 %copy-start.8 = (bf16[128,1664]{1,0:T(8,128)(2,1)S(1)}, bf16[128,1664]{1,0:T(8,128)(2,1)}, u32[]{:S(2)}) copy-start(bf16[128,1664]{1,0:T(8,128)(2,1)} %param.19) | copy-start | bytes 1277956
  7.2 6.4 %copy-start.4 = (bf16[128,1664]{1,0:T(8,128)(2,1)S(1)}, bf16[128,1664]{1,0:T(8,128)(2,1)}, u32[]{:S(2)}) copy-start(bf16[128,1664]{1,0:T(8,128)(2,1)} %param.20) | copy-start | bytes 1277956
  7.2 10.0 %copy-start.6 = (bf16[128,1664]{1,0:T(8,128)(2,1)S(1)}, bf16[128,1664]{1,0:T(8,128)(2,1)}, u32[]{:S(2)}) copy-start(bf16[128,1664]{1,0:T(8,128)(2,1)} %param.21) | copy-start | bytes 1277956
  7.2 339.0 %reduce-scatter.2.cloned.1.call-start = ((), (), s32[]{:S(2)}) async-start(), calls=%async_computation.3 | async-start | bytes 14057472 | tf_op jit(solution)/shard_map/reduce_scatter | solution.py:92
  7.3 17.5 %copy-start.10 = (s32[4096]{0:T(1024)S(1)}, s32[4096]{0:T(1024)}, u32[]{:S(2)}) copy-start(s32[4096]{0:T(1024)} %param.22) | copy-start | bytes 49156
  14.5 15.2 %copy-start.3 = (bf16[128,1664]{1,0:T(8,128)(2,1)}, bf16[128,1664]{1,0:T(8,128)(2,1)S(1)}, u32[]{:S(2)}) copy-start(bf16[128,1664]{1,0:T(8,128)(2,1)S(1)} %scatter_fusion) | copy-start | bytes 1277956
  14.5 10.5 %collective-permute-start.2 = (bf16[128,1664]{1,0:T(8,128)(2,1)S(1)}, bf16[128,1664]{1,0:T(8,128)(2,1)S(1)}, u32[]{:S(2)}, u32[]{:S(2)}) collective-permute-start(bf16[128,1664]{1,0:T(8,128)(2,1)S(1)} %scatter_fusion), channel_id=1, source_target_pairs={{0,4},{4,8},{8,12},{12,16},{16,20},{20,24},{24,28},{28,32},{32,36}... | collective-permute-start | bytes 1277960 | tf_op jit(solution)/shard_map/ppermute | solution.py:13
  15.9 9.9 %collective-permute-start.3 = (bf16[128,1664]{1,0:T(8,128)(2,1)S(1)}, bf16[128,1664]{1,0:T(8,128)(2,1)}, u32[]{:S(2)}, u32[]{:S(2)}) collective-permute-start(bf16[128,1664]{1,0:T(8,128)(2,1)S(1)} %scatter_fusion), channel_id=1, source_target_pairs={{4,0},{8,4},{12,8},{16,12},{20,16},{24,20},{28,24},{32,28},{36,32}... | collective-permute-start | bytes 1277960 | tf_op jit(solution)/shard_map/ppermute | solution.py:13
  17.2 11.4 %collective-permute-start = (bf16[128,1664]{1,0:T(8,128)(2,1)S(1)}, bf16[128,1664]{1,0:T(8,128)(2,1)S(1)}, u32[]{:S(2)}, u32[]{:S(2)}) collective-permute-start(bf16[128,1664]{1,0:T(8,128)(2,1)S(1)} %copy-done.6), channel_id=1, source_target_pairs={{0,4},{4,8},{8,12},{12,16},{16,20},{20,24},{24,28},{28,32},{32,36}... | collective-permute-start | bytes 1277960 | tf_op jit(solution)/shard_map/ppermute | solution.py:13
  22.4 6.1 %collective-permute-start.1 = (bf16[128,1664]{1,0:T(8,128)(2,1)S(1)}, bf16[128,1664]{1,0:T(8,128)(2,1)}, u32[]{:S(2)}, u32[]{:S(2)}) collective-permute-start(bf16[128,1664]{1,0:T(8,128)(2,1)S(1)} %copy-done.6), channel_id=1, source_target_pairs={{4,0},{8,4},{12,8},{16,12},{20,16},{24,20},{28,24},{32,28},{36,32}... | collective-permute-start | bytes 1277960 | tf_op jit(solution)/shard_map/ppermute | solution.py:13
  25.0 0.8 copy-start.7
  31.3 4.4 %copy-start.5 = (bf16[384,1664]{0,1:T(8,128)(2,1)S(1)}, bf16[384,1664]{0,1:T(8,128)(2,1)}, u32[]{:S(2)}) copy-start(bf16[384,1664]{0,1:T(8,128)(2,1)} %copy.30) | copy-start | bytes 3833860
  35.7 2.9 copy-start.2
  38.2 0.8 copy-start.11
  45.8 166.9 %copy-start.15 = (bf16[1664,256]{1,0:T(8,128)(2,1)S(1)}, bf16[1664,256]{1,0:T(8,128)(2,1)}, u32[]{:S(2)}) copy-start(bf16[1664,256]{1,0:T(8,128)(2,1)} %param.29) | copy-start | bytes 2555908
  45.8 166.9 %copy-start.16 = (f32[256]{0:T(256)S(1)}, f32[256]{0:T(256)}, u32[]{:S(2)}) copy-start(f32[256]{0:T(256)} %param.30) | copy-start | bytes 3076
  240.5 0.7 copy-start.14
  241.1 106.9 %copy-start.9 = (f32[1664]{0:T(1024)S(1)}, f32[1664]{0:T(1024)}, u32[]{:S(2)}) copy-start(f32[1664]{0:T(1024)} %param.32) | copy-start | bytes 19972
  241.1 107.3 %copy-start.12 = (f32[1664]{0:T(1024)S(1)}, f32[1664]{0:T(1024)}, u32[]{:S(2)}) copy-start(f32[1664]{0:T(1024)} %param.35) | copy-start | bytes 19972
  241.1 107.3 %copy-start.13 = (f32[1664]{0:T(1024)S(1)}, f32[1664]{0:T(1024)}, u32[]{:S(2)}) copy-start(f32[1664]{0:T(1024)} %param.33) | copy-start | bytes 19972
  347.6 17.1 %copy-start.1 = (bf16[256,1664]{1,0:T(8,128)(2,1)S(1)}, bf16[256,1664]{1,0:T(8,128)(2,1)}, u32[]{:S(2)}) copy-start(bf16[256,1664]{1,0:T(8,128)(2,1)} %param.31) | copy-start | bytes 2555908
Sparse Core Ops, SparseCore 0:
  240.6 105.4 reduce-scatter.1
